TPU v7x, 32 devices: a whole 2x2x4 slice. The times are simulated.
32 devices in a mesh: groups: 2 (over y), seq: 4 (over z), head: 2 (over x), sub: 2 (over core).
Axes of the slice: x: 2, y: 2, z: 4, core: 2. Of those that a mesh axis runs over, the one named last changes fastest.
Arguments:
- tokens: bfloat16 [4096, 3072], P(('groups', 'seq')), parts along dimension 0, may hold values from -6 to 6
- modulation: float32 [3, 3072], replicated, may hold values from -4 to 4
- w_qkv: bfloat16 [3072, 8, 768], P('seq', ('head', 'sub')), may hold values from -0.15625 to 0.15625
- w_out: bfloat16 [2048, 3072], P('seq', ('head', 'sub')), may hold values from -0.125 to 0.125
- pattern: int32 [32, 4], P(('groups', 'seq')), parts along dimension 0, may hold values from 0 to 15, as said below
- counts: int32 [32], P(('groups', 'seq')), parts along dimension 0, may hold values from 1 to 4, as said below
- spatial_mask: int32 [8, 4, 4], P(('groups', 'seq')), parts along dimension 0, may hold values from 0 to 1, as said below
Outputs:
- update: bfloat16 [4096, 3072], P(('groups', 'seq'), ('head', 'sub')), parts along dimension 0
There are 2 independent parts, one for each index of `groups`. A program takes and returns all parts, laid end to end along the dimension named above; an argument that names none is the same for every part. Nothing has to cross between parts.
Inputs may be any that keep to these rules, and one draw needn't show every extreme that they name: pattern[b, 0] = b; each further entry of row b is b plus a nonzero offset of size at most 2, the offsets of one row different, clipped to the blocks of the video. `counts`: blocks with a count above one all lie in one cyclic run of half of the 16 blocks. `spatial_mask`: every diagonal entry is 1.
All inputs are finite; a program needn't handle non-finite values.
Results may differ from a plain program's by a relative error of at most 0.012.
The roundings to bfloat16 on the way count: a program that leaves them out, or rounds other values in their place, can miss the bound.
Values may be sent and summed in bfloat16 or wider, within the bound.
A program may use at most 128 MiB of HBM per device.

v0:
```python
import math
import jax
import jax.numpy as jnp
from jax import lax
from jax.sharding import PartitionSpec as P

BLOCK = 128
WIN = 2
EPSILON = 1e-06


def with_halo(cells, sides, width):
    for axis, dim in sides:
        count = lax.axis_size(axis)
        ends = count - 1
        head = lax.slice_in_dim(cells, 0, width, axis=dim)
        tail = lax.slice_in_dim(cells, cells.shape[dim] - width, cells.shape[dim], axis=dim)
        cells = jnp.concatenate(
            [
                lax.ppermute(tail, axis, [(i, (i + 1) % count) for i in range(ends)]),
                cells,
                lax.ppermute(head, axis, [((i + 1) % count, i) for i in range(ends)]),
            ],
            axis=dim,
        )
    return cells


def modulate(tokens, modulation):
    values = tokens.astype(jnp.float32)
    center = jnp.mean(values, axis=-1, keepdims=True)
    spread = jnp.mean(jnp.square(values - center), axis=-1, keepdims=True)
    normed = (values - center) * lax.rsqrt(spread + EPSILON)
    return (normed * (1.0 + modulation[1]) + modulation[0]).astype(jnp.bfloat16)


def shards(tokens, modulation, w_qkv, w_out, pattern, counts, spatial_mask):
    row_count, feature_width = tokens.shape
    pairs_local = w_qkv.shape[1]
    head_size = w_qkv.shape[2] // 6
    frames_local = spatial_mask.shape[0]
    positions = row_count // frames_local
    slot_total = pattern.shape[1]
    scale_factor = 1.0 / math.sqrt(head_size)
    hidden = modulate(tokens, modulation)
    piece = lax.all_gather(w_qkv, "seq", axis=0, tiled=True)
    projected = jnp.dot(
        hidden, piece.reshape(piece.shape[0], -1), preferred_element_type=jnp.float32
    )
    whole_out = lax.all_gather(w_out, "seq", axis=0, tiled=True)
    packed = projected.astype(jnp.bfloat16).reshape(
        frames_local, positions, pairs_local, 6 * head_size
    )
    temporal_in = packed[..., : 3 * head_size].transpose(1, 0, 2, 3)
    received = lax.all_to_all(temporal_in, "seq", split_axis=0, concat_axis=1, tiled=True)
    position_span, frame_total, items, _ = received.shape
    relaid = received.reshape(position_span * frame_total, items, 3 * head_size)
    extended = with_halo(relaid[:, :, head_size:], (("seq", 0),), WIN * BLOCK)
    block_count = position_span * frame_total // BLOCK
    key_table = extended.reshape(block_count + 2 * WIN, BLOCK, items, 2 * head_size)
    queries = relaid[:, :, :head_size].reshape(block_count, BLOCK, items, head_size)
    offsets = pattern - (lax.axis_index("seq") * block_count - WIN)

    def slot_step(slot_index, state_pair):
        numerator, denominator = state_pair
        chosen = lax.dynamic_index_in_dim(offsets, slot_index, 1, keepdims=False)
        picked = jnp.take(key_table, chosen, axis=0)
        scores = (
            jnp.einsum(
                "bqnc,bknc->bnqk",
                queries,
                picked[..., :head_size],
                preferred_element_type=jnp.float32,
            )
            * scale_factor
        )
        alive = (slot_index < counts).astype(jnp.float32)
        weights = jnp.exp(scores) * alive[:, None, None, None]
        numerator = numerator + jnp.einsum(
            "bnqk,bknc->bnqc",
            weights.astype(jnp.bfloat16),
            picked[..., head_size:],
            preferred_element_type=jnp.float32,
        )
        return (numerator, denominator + jnp.sum(weights, axis=-1))

    start_state = (
        jnp.zeros((block_count, items, BLOCK, head_size), jnp.float32),
        jnp.zeros((block_count, items, BLOCK), jnp.float32),
    )
    numerator, denominator = lax.fori_loop(0, slot_total, slot_step, start_state)
    outcome = (numerator / denominator[..., None]).astype(jnp.bfloat16)
    outcome = outcome.transpose(0, 2, 1, 3).reshape(position_span, frame_total, items, head_size)
    temporal_out = lax.all_to_all(outcome, "seq", split_axis=1, concat_axis=0, tiled=True)
    spatial = packed[..., 3 * head_size :]
    blocks_frame = positions // BLOCK
    scores = (
        jnp.einsum(
            "fpnc,fqnc->fnpq",
            spatial[..., :head_size],
            spatial[..., head_size : 2 * head_size],
            preferred_element_type=jnp.float32,
        )
        * scale_factor
    )
    keep = spatial_mask.astype(jnp.float32)[:, None, :, None, :, None]
    weights = (
        jnp.exp(scores).reshape(frames_local, pairs_local, blocks_frame, BLOCK, blocks_frame, BLOCK)
        * keep
    )
    weights = weights.reshape(frames_local, pairs_local, positions, positions)
    denominator = jnp.sum(weights, axis=-1)
    numerator = jnp.einsum(
        "fnpq,fqnc->fpnc",
        weights.astype(jnp.bfloat16),
        spatial[..., 2 * head_size :],
        preferred_element_type=jnp.float32,
    )
    spatial_out = (numerator / denominator.transpose(0, 2, 1)[..., None]).astype(jnp.bfloat16)
    attention = jnp.concatenate([temporal_out.transpose(1, 0, 2, 3), spatial_out], axis=-1)
    attention = attention.reshape(row_count, pairs_local, 2 * head_size)
    out_width = whole_out.shape[1]
    mixed = jnp.dot(
        lax.all_gather(attention, ("head", "sub"), axis=1, tiled=True).reshape(row_count, -1),
        whole_out,
        preferred_element_type=jnp.float32,
    )
    gate_slice = lax.dynamic_slice_in_dim(
        modulation[2], lax.axis_index(("head", "sub")) * out_width, out_width, 0
    )
    return (gate_slice * mixed).astype(jnp.bfloat16)


def solution(mesh):
    return jax.shard_map(
        shards,
        mesh=mesh,
        in_specs=(
            P(("groups", "seq"), None),
            P(),
            P("seq", ("head", "sub"), None),
            P("seq", ("head", "sub")),
            P(("groups", "seq"), None),
            P(("groups", "seq")),
            P(("groups", "seq"), None, None),
        ),
        out_specs=P(("groups", "seq"), ("head", "sub")),
        check_vma=False,
    )
```

profile of v0, /device:TPU:0, one launch (start us, length us, event | category | flops | bytes accessed | tf_op | source)
XLA Modules:
  0.0 360.5 jit_solution(18314034296797499365)
XLA Ops:
  7.3 2.6 convert_reduce_fusion
  10.9 167.5 %all-gather.5.cloned.1.call-done = bf16[3072,2,768]{2,1,0:T(2,128)(2,1)} async-done(((bf16[768,2,768]{2,1,0:T(2,128)(2,1)}), bf16[3072,2,768]{2,1,0:T(2,128)(2,1)}) %all-gather.5.cloned.1.call-update) | async-done | bytes 9437200 | tf_op jit(solution)/shard_map/all_gather | solution.py:46
  178.4 9.0 %copy.65 = bf16[384,8,2,768]{3,1,2,0:T(8,128)(2,1)} copy(bf16[384,8,2,768]{3,2,1,0:T(2,128)(2,1)} %bitcast.76) | data formatting | bytes 18874368
  187.4 10.0 %fusion.18 = bf16[512,1536]{1,0:T(8,128)(2,1)} fusion(bf16[3072,1536]{1,0:T(8,128)(2,1)} %bitcast.77, bf16[512,3072]{1,0:T(8,128)(2,1)S(1)} %copy-done, f32[3072]{0:T(1024)S(1)} %bitcast.89, f32[3072]{0:T(1024)S(1)} %bitcast.90, f32[512]{0:T(512)S(1)} %add_rsqrt_fusion, f32[512]{0:T(512)S(1)} %broadcast_multiply_fusion), kind=kOutput, calls=%fused_computation.28 | convolution fusion | flops 4842061824 | bytes 14184448 | tf_op jit(solution)/shard_map/dot_general | solution.py:47
  197.4 3.6 %reshape.85 = bf16[1,512,2,768]{3,2,1,0:T(2,128)(2,1)S(1)} reshape(bf16[512,1536]{1,0:T(8,128)(2,1)} %fusion.18) | data formatting | bytes 3145728 | tf_op jit(solution)/shard_map/reshape | solution.py:51
  201.1 1.4 slice_bitcast_fusion
  202.5 3.5 all-to-all-start
  206.1 20.4 %all-to-all-done = bf16[512,1,2,384]{3,2,1,0:T(2,128)(2,1)S(1)} async-done(((bf16[512,1,2,384]{3,2,1,0:T(2,128)(2,1)}), bf16[512,1,2,384]{3,2,1,0:T(2,128)(2,1)S(1)}, u32[]{:S(2)}, u32[]{:S(2)}) %all-to-all-start) | async-done | bytes 786464 | tf_op jit(solution)/shard_map/all_to_all | solution.py:55
  226.5 1.5 copy.81
  228.0 1.6 reshape.86
  230.5 2.0 collective-permute-start
  232.5 1.3 collective-permute-start.1
  235.1 1.2 fusion.33
  237.2 4.8 %collective-permute-done.1 = bf16[256,2,256]{2,0,1:T(8,128)(2,1)} collective-permute-done((bf16[256,2,256]{2,0,1:T(8,128)(2,1)}, bf16[256,2,256]{2,0,1:T(8,128)(2,1)}, u32[]{:S(2)}, u32[]{:S(2)}) %collective-permute-start.1) | collective-permute-done | bytes 262176 | tf_op jit(solution)/shard_map/ppermute | solution.py:22
  242.0 1.1 pad_maximum_fusion
  243.2 5.9 %while.16 = (s32[]{:T(128)}, f32[4,2,128,128]{3,2,1,0:T(8,128)S(1)}, f32[4,2,128]{2,1,0:T(2,128)S(1)}, s32[4,4]{0,1:T(4,128)S(1)}, bf16[8,128,2,256]{3,1,2,0:T(8...) while((s32[]{:T(128)}, ...), condition=%wide.region_4.5_spmd.clone, body=%wide.region_2.4_spmd.clone.sunk | while | flops 68159520 | bytes 4477664 | solution.py:91
  250.2 3.4 all-to-all-start.1
  253.8 1.9 fusion.21
  255.9 2.1 fusion.24
  258.0 3.4 all-to-all-done.1
  263.5 20.8 %all-gather.9.cloned.1.call-done = bf16[1,512,8,256]{3,1,0,2:T(8,128)(2,1)} async-done(((bf16[1,512,2,256]{3,1,0,2:T(8,128)(2,1)}), bf16[1,512,8,256]{3,1,0,2:T(8,128)(2,1)}) %all-gather.9.cloned.1.call-update) | async-done | bytes 2097168 | tf_op jit(solution)/shard_map/all_gather | solution.py:124
  284.3 2.9 copy.59
  287.2 62.2 %all-gather.7.cloned.1.call-done = bf16[2048,768]{1,0:T(8,128)(2,1)} async-done(((bf16[512,768]{1,0:T(8,128)(2,1)}), bf16[2048,768]{1,0:T(8,128)(2,1)}) %all-gather.7.cloned.1.call-update) | async-done | bytes 3145744 | tf_op jit(solution)/shard_map/all_gather | solution.py:50
  349.3 4.6 %multiply_convert_fusion = bf16[512,768]{1,0:T(8,128)(2,1)} fusion(bf16[512,2048]{0,1:T(8,128)(2,1)S(1)} %bitcast.84, bf16[2048,768]{1,0:T(8,128)(2,1)} %all-gather.7.cloned.1.call-done, f32[768]{0:T(1024)S(1)} %dynamic-slice_reduce_fusion), kind=kOutput, calls=%fused_computation.32 | convolution fusion | flops 1611399168 | bytes 6032384 | tf_op jit(solution)/shard_map/dot_general | solution.py:123
  (79 shorter events, 14.1 us)
Async XLA Ops:
  6.5 171.9 %all-gather.5.cloned.1.call-start = ((), (), s32[]{:S(2)}) async-start(), calls=%async_computation.2 | async-start | bytes 11796480 | tf_op jit(solution)/shard_map/all_gather | solution.py:46
  6.5 3.3 copy-start
  9.9 1.0 copy-start.3
  201.0 5.0 %copy-start.4 = (s32[4,4]{1,0:T(4,128)S(1)}, s32[4,4]{1,0:T(4,128)}, u32[]{:S(2)}) copy-start(s32[4,4]{1,0:T(4,128)} %param.13) | copy-start | bytes 196
  201.1 5.0 %copy-start.5 = (s32[1,4,4]{2,1,0:T(4,128)S(1)}, s32[1,4,4]{2,1,0:T(4,128)}, u32[]{:S(2)}) copy-start(s32[1,4,4]{2,1,0:T(4,128)} %param.15) | copy-start | bytes 196
  202.5 24.0 %all-to-all-start = ((bf16[512,1,2,384]{3,2,1,0:T(2,128)(2,1)}), bf16[512,1,2,384]{3,2,1,0:T(2,128)(2,1)S(1)}, u32[]{:S(2)}, u32[]{:S(2)}) async-start(bf16[512,1,2,384]{3,2,1,0:T(2,128)(2,1)} %slice_bitcast_fusion), calls=%async_computation | async-start | bytes 1572864 | tf_op jit(solution)/shard_map/all_to_all | solution.py:55
  230.5 6.8 %collective-permute-start = (bf16[256,2,256]{2,0,1:T(8,128)(2,1)}, bf16[256,2,256]{2,0,1:T(8,128)(2,1)}, u32[]{:S(2)}, u32[]{:S(2)}) collective-permute-start(bf16[256,2,256]{2,0,1:T(8,128)(2,1)} %get-tuple-element.198), channel_id=1, source_target_pairs={{0,4},{4,8},{8,12},{1,5},{5,9},{9,13},{2,6},{6,10},{10,14},{3,7},{... | collective-permute-start | bytes 786440 | tf_op jit(solution)/shard_map/ppermute | solution.py:20
  232.5 9.6 %collective-permute-start.1 = (bf16[256,2,256]{2,0,1:T(8,128)(2,1)}, bf16[256,2,256]{2,0,1:T(8,128)(2,1)}, u32[]{:S(2)}, u32[]{:S(2)}) collective-permute-start(bf16[256,2,256]{2,0,1:T(8,128)(2,1)} %get-tuple-element.199), channel_id=1, source_target_pairs={{4,0},{8,4},{12,8},{5,1},{9,5},{13,9},{6,2},{10,6},{14,10},{7,3},{... | collective-permute-start | bytes 786440 | tf_op jit(solution)/shard_map/ppermute | solution.py:22
  236.4 6.8 %copy-start.6 = (s32[4]{0:T(128)S(1)}, s32[4]{0:T(128)}, u32[]{:S(2)}) copy-start(s32[4]{0:T(128)} %param.14) | copy-start | bytes 52
  249.2 4.6 %copy-start.1 = (f32[64,8,4,128]{3,1,2,0:T(8,128)S(1)}, f32[64,8,4,128]{3,1,2,0:T(8,128)}, u32[]{:S(2)}) copy-start(f32[64,8,4,128]{3,1,2,0:T(8,128)} %copy.80) | copy-start | bytes 3145732
  249.4 6.3 %copy-start.2 = (bf16[1,512,2,128]{3,2,1,0:T(2,128)(2,1)S(1)}, bf16[1,512,2,128]{3,2,1,0:T(2,128)(2,1)}, u32[]{:S(2)}) copy-start(bf16[1,512,2,128]{3,2,1,0:T(2,128)(2,1)} %get-tuple-element.195) | copy-start | bytes 786436
  250.2 11.2 %all-to-all-start.1 = ((bf16[128,4,2,128]{3,0,2,1:T(8,128)(2,1)}), bf16[128,4,2,128]{3,0,2,1:T(8,128)(2,1)S(1)}, u32[]{:S(2)}, u32[]{:S(2)}) async-start(bf16[128,4,2,128]{3,0,2,1:T(8,128)(2,1)} %copy.51), calls=%async_computation.1 | async-start | bytes 524288 | tf_op jit(solution)/shard_map/all_to_all | solution.py:94
  253.6 30.7 %all-gather.9.cloned.1.call-start = ((), (), s32[]{:S(2)}) async-start(), calls=%async_computation.4 | async-start | bytes 2621440 | tf_op jit(solution)/shard_map/all_gather | solution.py:124
  262.8 86.6 %all-gather.7.cloned.1.call-start = ((), (), s32[]{:S(2)}) async-start(), calls=%async_computation.3 | async-start | bytes 3932160 | tf_op jit(solution)/shard_map/all_gather | solution.py:50
Sparse Core Ops, SparseCore 0:
  8.9 169.4 all-gather.4
  262.9 21.3 all-gather.8
  285.9 63.4 all-gather.6
where the time goes:
time: 361 us; the launch traced here: 360 us
  waiting for transfers between devices  281 us (78%)
  local copies, waits for them, and re-layouts  28.3 us (8%)
  matrix products  21.3 us (6%)
  between operations  13.4 us (4%)
  starting transfers between devices  10.5 us (3%)
  other arithmetic  5.58 us (2%)
    all_gather x1, waiting for transfers between devices, shards(): piece = lax.all_gather(w_qkv, 'seq', axis=0, tiled=True)  168 us
    all_gather x1, waiting for transfers between devices, shards(): whole_out = lax.all_gather(w_out, 'seq', axis=0, tiled=True)  62.2 us
    all_gather x1, waiting for transfers between devices, shards(): lax.all_gather(attention, ('head', 'sub'), axis=1, tiled=True)  20.8 us
    all_to_all x1, waiting for transfers between devices, shards(): lax.all_to_all(temporal_in, 'seq', split_axis=0, concat_axis=1, tiled=True)  20.4 us
    unnamed x20, local copies, waits for them, and re-layouts  10.5 us
    dot_general x1, matrix products, shards(): jnp.dot(hidden, piece.reshape(piece.shape[0], -1), preferred_element_type...  10 us
  transfers between devices with their start and end apart: 7, of which 7 were waited for; matrix products, arithmetic and copies ran while one was open for 4% of the time, Pallas kernels for 0%

commit v1 on v0

--- a/solution.py
+++ b/solution.py
@@ -121,7 +121,7 @@
     attention = attention.reshape(row_count, pairs_local, 2 * head_size)
     out_width = whole_out.shape[1]
     mixed = jnp.dot(
-        lax.all_gather(attention, ("head", "sub"), axis=1, tiled=True).reshape(row_count, -1),
+        jnp.concatenate(lax.all_gather(attention, ("head", "sub")), axis=1).reshape(row_count, -1),
         whole_out,
         preferred_element_type=jnp.float32,
     )

time: 361 us -> 361 us (level)
  no operation moved by 1% of the time
where the time goes in v1:
time: 361 us; the launch traced here: 360 us
  waiting for transfers between devices  281 us (78%)
  local copies, waits for them, and re-layouts  28.2 us (8%)
  matrix products  21.3 us (6%)
  between operations  13.4 us (4%)
  starting transfers between devices  10.5 us (3%)
  other arithmetic  5.58 us (2%)
    all_gather x1, waiting for transfers between devices, shards(): piece = lax.all_gather(w_qkv, 'seq', axis=0, tiled=True)  168 us
    all_gather x1, waiting for transfers between devices, shards(): whole_out = lax.all_gather(w_out, 'seq', axis=0, tiled=True)  62.3 us
    all_gather x1, waiting for transfers between devices, shards(): lax.all_gather(attention, ('head', 'sub'))  20.8 us
    all_to_all x1, waiting for transfers between devices, shards(): lax.all_to_all(temporal_in, 'seq', split_axis=0, concat_axis=1, tiled=True)  20.4 us
    unnamed x20, local copies, waits for them, and re-layouts  10.5 us
    dot_general x1, matrix products, shards(): jnp.dot(hidden, piece.reshape(piece.shape[0], -1), preferred_element_type...  10 us
  transfers between devices with their start and end apart: 7, of which 7 were waited for; matrix products, arithmetic and copies ran while one was open for 4% of the time, Pallas kernels for 0%

profile of v1, /device:TPU:0, one launch (start us, length us, event | category | flops | bytes accessed | tf_op | source)
XLA Modules:
  0.0 360.5 jit_solution(11769321107834531793)
XLA Ops:
  7.3 2.6 convert_reduce_fusion
  10.9 167.5 %all-gather.4.cloned.1.call-done = bf16[3072,2,768]{2,1,0:T(2,128)(2,1)} async-done(((bf16[768,2,768]{2,1,0:T(2,128)(2,1)}), bf16[3072,2,768]{2,1,0:T(2,128)(2,1)}) %all-gather.4.cloned.1.call-update) | async-done | bytes 9437200 | tf_op jit(solution)/shard_map/all_gather | solution.py:46
  178.4 9.0 %copy.65 = bf16[384,8,2,768]{3,1,2,0:T(8,128)(2,1)} copy(bf16[384,8,2,768]{3,2,1,0:T(2,128)(2,1)} %bitcast.78) | data formatting | bytes 18874368
  187.4 10.0 %fusion.18 = bf16[512,1536]{1,0:T(8,128)(2,1)} fusion(bf16[3072,1536]{1,0:T(8,128)(2,1)} %bitcast.79, bf16[512,3072]{1,0:T(8,128)(2,1)S(1)} %copy-done, f32[3072]{0:T(1024)S(1)} %bitcast.91, f32[3072]{0:T(1024)S(1)} %bitcast.92, f32[512]{0:T(512)S(1)} %add_rsqrt_fusion, f32[512]{0:T(512)S(1)} %broadcast_multiply_fusion), kind=kOutput, calls=%fused_computation.28 | convolution fusion | flops 4842061824 | bytes 14184448 | tf_op jit(solution)/shard_map/dot_general | solution.py:47
  197.4 3.6 %reshape.82 = bf16[1,512,2,768]{3,2,1,0:T(2,128)(2,1)S(1)} reshape(bf16[512,1536]{1,0:T(8,128)(2,1)} %fusion.18) | data formatting | bytes 3145728 | tf_op jit(solution)/shard_map/reshape | solution.py:51
  201.1 1.4 slice_bitcast_fusion
  202.5 3.5 all-to-all-start
  206.1 20.4 %all-to-all-done = bf16[512,1,2,384]{3,2,1,0:T(2,128)(2,1)S(1)} async-done(((bf16[512,1,2,384]{3,2,1,0:T(2,128)(2,1)}), bf16[512,1,2,384]{3,2,1,0:T(2,128)(2,1)S(1)}, u32[]{:S(2)}, u32[]{:S(2)}) %all-to-all-start) | async-done | bytes 786464 | tf_op jit(solution)/shard_map/all_to_all | solution.py:55
  226.5 1.5 copy.81
  228.0 1.6 reshape.83
  230.5 2.0 collective-permute-start
  232.5 1.3 collective-permute-start.1
  235.1 1.2 fusion.33
  237.2 4.8 %collective-permute-done.1 = bf16[256,2,256]{2,0,1:T(8,128)(2,1)} collective-permute-done((bf16[256,2,256]{2,0,1:T(8,128)(2,1)}, bf16[256,2,256]{2,0,1:T(8,128)(2,1)}, u32[]{:S(2)}, u32[]{:S(2)}) %collective-permute-start.1) | collective-permute-done | bytes 262176 | tf_op jit(solution)/shard_map/ppermute | solution.py:22
  242.0 1.1 pad_maximum_fusion
  243.2 5.9 %while.16 = (s32[]{:T(128)}, f32[4,2,128,128]{3,2,1,0:T(8,128)S(1)}, f32[4,2,128]{2,1,0:T(2,128)S(1)}, s32[4,4]{0,1:T(4,128)S(1)}, bf16[8,128,2,256]{3,1,2,0:T(8...) while((s32[]{:T(128)}, ...), condition=%wide.region_4.5_spmd.clone, body=%wide.region_2.4_spmd.clone.sunk | while | flops 68159520 | bytes 4477664 | solution.py:91
  250.2 3.4 all-to-all-start.1
  253.8 1.9 fusion.21
  255.9 2.1 fusion.24
  258.0 3.4 all-to-all-done.1
  263.5 20.8 %all-gather.6.cloned.1.call-done = bf16[4,512,2,256]{3,1,2,0:T(8,128)(2,1)} async-done(((bf16[1,512,2,256]{3,1,2,0:T(8,128)(2,1)}), bf16[4,512,2,256]{3,1,2,0:T(8,128)(2,1)}) %all-gather.6.cloned.1.call-update) | async-done | bytes 2097168 | tf_op jit(solution)/shard_map/all_gather | solution.py:124
  284.3 2.8 copy.59
  287.1 62.3 %all-gather.8.cloned.1.call-done = bf16[2048,768]{1,0:T(8,128)(2,1)} async-done(((bf16[512,768]{1,0:T(8,128)(2,1)}), bf16[2048,768]{1,0:T(8,128)(2,1)}) %all-gather.8.cloned.1.call-update) | async-done | bytes 3145744 | tf_op jit(solution)/shard_map/all_gather | solution.py:50
  349.3 4.6 %multiply_convert_fusion = bf16[512,768]{1,0:T(8,128)(2,1)} fusion(bf16[512,2048]{0,1:T(8,128)(2,1)S(1)} %bitcast.86, bf16[2048,768]{1,0:T(8,128)(2,1)} %all-gather.8.cloned.1.call-done, f32[768]{0:T(1024)S(1)} %dynamic-slice_reduce_fusion), kind=kOutput, calls=%fused_computation.32 | convolution fusion | flops 1611399168 | bytes 6032384 | tf_op jit(solution)/shard_map/dot_general | solution.py:123
  (79 shorter events, 14.1 us)
Async XLA Ops:
  6.5 171.9 %all-gather.4.cloned.1.call-start = ((), (), s32[]{:S(2)}) async-start(), calls=%async_computation.2 | async-start | bytes 11796480 | tf_op jit(solution)/shard_map/all_gather | solution.py:46
  6.5 3.3 copy-start
  9.9 1.0 copy-start.3
  201.0 5.0 %copy-start.4 = (s32[4,4]{1,0:T(4,128)S(1)}, s32[4,4]{1,0:T(4,128)}, u32[]{:S(2)}) copy-start(s32[4,4]{1,0:T(4,128)} %param.13) | copy-start | bytes 196
  201.1 5.0 %copy-start.5 = (s32[1,4,4]{2,1,0:T(4,128)S(1)}, s32[1,4,4]{2,1,0:T(4,128)}, u32[]{:S(2)}) copy-start(s32[1,4,4]{2,1,0:T(4,128)} %param.15) | copy-start | bytes 196
  202.5 24.0 %all-to-all-start = ((bf16[512,1,2,384]{3,2,1,0:T(2,128)(2,1)}), bf16[512,1,2,384]{3,2,1,0:T(2,128)(2,1)S(1)}, u32[]{:S(2)}, u32[]{:S(2)}) async-start(bf16[512,1,2,384]{3,2,1,0:T(2,128)(2,1)} %slice_bitcast_fusion), calls=%async_computation | async-start | bytes 1572864 | tf_op jit(solution)/shard_map/all_to_all | solution.py:55
  230.5 6.8 %collective-permute-start = (bf16[256,2,256]{2,0,1:T(8,128)(2,1)}, bf16[256,2,256]{2,0,1:T(8,128)(2,1)}, u32[]{:S(2)}, u32[]{:S(2)}) collective-permute-start(bf16[256,2,256]{2,0,1:T(8,128)(2,1)} %get-tuple-element.198), channel_id=1, source_target_pairs={{0,4},{4,8},{8,12},{1,5},{5,9},{9,13},{2,6},{6,10},{10,14},{3,7},{... | collective-permute-start | bytes 786440 | tf_op jit(solution)/shard_map/ppermute | solution.py:20
  232.5 9.6 %collective-permute-start.1 = (bf16[256,2,256]{2,0,1:T(8,128)(2,1)}, bf16[256,2,256]{2,0,1:T(8,128)(2,1)}, u32[]{:S(2)}, u32[]{:S(2)}) collective-permute-start(bf16[256,2,256]{2,0,1:T(8,128)(2,1)} %get-tuple-element.199), channel_id=1, source_target_pairs={{4,0},{8,4},{12,8},{5,1},{9,5},{13,9},{6,2},{10,6},{14,10},{7,3},{... | collective-permute-start | bytes 786440 | tf_op jit(solution)/shard_map/ppermute | solution.py:22
  236.4 6.8 %copy-start.6 = (s32[4]{0:T(128)S(1)}, s32[4]{0:T(128)}, u32[]{:S(2)}) copy-start(s32[4]{0:T(128)} %param.14) | copy-start | bytes 52
  249.2 4.6 %copy-start.1 = (f32[64,8,4,128]{3,1,2,0:T(8,128)S(1)}, f32[64,8,4,128]{3,1,2,0:T(8,128)}, u32[]{:S(2)}) copy-start(f32[64,8,4,128]{3,1,2,0:T(8,128)} %copy.80) | copy-start | bytes 3145732
  249.4 6.3 %copy-start.2 = (bf16[1,512,2,128]{3,2,1,0:T(2,128)(2,1)S(1)}, bf16[1,512,2,128]{3,2,1,0:T(2,128)(2,1)}, u32[]{:S(2)}) copy-start(bf16[1,512,2,128]{3,2,1,0:T(2,128)(2,1)} %get-tuple-element.195) | copy-start | bytes 786436
  250.2 11.2 %all-to-all-start.1 = ((bf16[128,4,2,128]{3,0,2,1:T(8,128)(2,1)}), bf16[128,4,2,128]{3,0,2,1:T(8,128)(2,1)S(1)}, u32[]{:S(2)}, u32[]{:S(2)}) async-start(bf16[128,4,2,128]{3,0,2,1:T(8,128)(2,1)} %copy.51), calls=%async_computation.1 | async-start | bytes 524288 | tf_op jit(solution)/shard_map/all_to_all | solution.py:94
  253.6 30.7 %all-gather.6.cloned.1.call-start = ((), (), s32[]{:S(2)}) async-start(), calls=%async_computation.3 | async-start | bytes 2621440 | tf_op jit(solution)/shard_map/all_gather | solution.py:124
  262.8 86.6 %all-gather.8.cloned.1.call-start = ((), (), s32[]{:S(2)}) async-start(), calls=%async_computation.4 | async-start | bytes 3932160 | tf_op jit(solution)/shard_map/all_gather | solution.py:50
Sparse Core Ops, SparseCore 0:
  8.9 169.4 all-gather.3
  262.9 21.3 all-gather.5
  285.9 63.4 all-gather.7
